TPU v7x, 256 devices: a whole 4x4x8 slice. The times are simulated.
256 devices in a mesh: cluster: 32 (over z, y), group: 8 (over x, core).
Axes of the slice: x: 4, y: 4, z: 8, core: 2. Of those that a mesh axis runs over, the one named last changes fastest.
Arguments:
- loads: bfloat16 [512, 131072], P('group', 'cluster'), may hold values from -6 to 6
- near_blocks: bfloat16 [512, 24, 256, 256], P('cluster', 'group'), may hold values from -0.078125 to 0.078125
- near_cols: int32 [512, 24], P('cluster'), may hold values from 0 to 511, as said below
- far_right: bfloat16 [512, 64, 256], P('cluster'), may hold values from -0.375 to 0.375
- far_coupling: bfloat16 [512, 64, 1024], P('cluster'), may hold values from -0.1875 to 0.1875
- far_left: bfloat16 [512, 64, 256], P('cluster'), may hold values from -0.75 to 0.75
- far_cols: int32 [512, 16], P('cluster'), may hold values from 0 to 511, as said below
Outputs:
- response: bfloat16 [512, 131072], P('group', 'cluster')
Inputs may be any that keep to these rules, and one draw needn't show every extreme that they name: `near_cols`: the 24 entries of a row are distinct leaves i + d modulo 512, with |d| <= 16, for row leaf i. `far_cols`: the 16 entries of a row are distinct leaves i + d modulo 512, with 16 < d < 496, for row leaf i.
All inputs are finite; a program needn't handle non-finite values.
Results may differ from a plain program's by a relative error of at most 0.0049.
Values may be sent and summed in bfloat16 or wider, within the bound.
No kernel may reach another device: no remote copies, remote signals or barrier semaphores. Data moves between devices by JAX's collectives and lax.ppermute only.
A program may use at most 128 MiB of HBM per device.

v0:
```python
import jax
import jax.numpy as jnp
from jax import lax
from jax.sharding import PartitionSpec as P

REACH = 16


def with_halo(cells, sides, width):
    for axis, dim in sides:
        count = lax.axis_size(axis)
        head = lax.slice_in_dim(cells, 0, width, axis=dim)
        tail = lax.slice_in_dim(cells, cells.shape[dim] - width, cells.shape[dim], axis=dim)
        cells = jnp.concatenate(
            [
                lax.ppermute(tail, axis, [(i, (i + 1) % count) for i in range(count)]),
                cells,
                lax.ppermute(head, axis, [((i + 1) % count, i) for i in range(count)]),
            ],
            axis=dim,
        )
    return cells


def local(loads, near_blocks, near_cols, far_right, far_coupling, far_left, far_cols):
    columns = loads.shape[0]
    leaf_count = near_blocks.shape[0]
    per_group = near_blocks.shape[1]
    leaf = near_blocks.shape[2]
    rank = far_right.shape[1]
    far_count = far_cols.shape[1]
    total_leaves = leaf_count * lax.axis_size("cluster")
    cluster_id = lax.axis_index("cluster")
    group_id = lax.axis_index("group")
    gathered = lax.all_gather(loads, "group", axis=0, tiled=True)
    patterns = gathered.shape[0]
    widened = with_halo(gathered, (("cluster", 1),), REACH * leaf)
    wide_leaves = leaf_count + 2 * REACH
    wide_view = widened.reshape(patterns, wide_leaves, leaf)
    first_leaf = cluster_id * leaf_count - REACH
    leaf_ids = lax.dynamic_slice_in_dim(near_cols, group_id * per_group, per_group, 1)
    position = (leaf_ids - first_leaf) % total_leaves
    picked = jnp.take(wide_view, position, axis=1)
    result = jnp.einsum("rmkc,mknc->rmn", picked, near_blocks, preferred_element_type=jnp.float32)
    partial_value = result.reshape(patterns, near_blocks.shape[0] * leaf)
    near = lax.psum_scatter(partial_value, "group", scatter_dimension=0, tiled=True)
    own_loads = loads.reshape(columns, leaf_count, leaf)
    coef = jnp.einsum("rlc,lac->lra", own_loads, far_right, preferred_element_type=jnp.float32)
    coef = coef.astype(jnp.bfloat16).reshape(leaf_count, columns * rank)
    coupling = far_coupling.reshape(leaf_count, rank, far_count, rank)
    every_coef = lax.all_gather(coef, "cluster", axis=0, tiled=True)
    chosen = jnp.take(every_coef, far_cols, axis=0)
    chosen = chosen.reshape(leaf_count, far_count, columns, rank)
    reduced = jnp.einsum("lkra,lakb->lrb", chosen, coupling, preferred_element_type=jnp.float32)
    reduced = reduced.astype(jnp.bfloat16)
    far = jnp.einsum("lrb,lbn->rln", reduced, far_left, preferred_element_type=jnp.float32)
    far = far.reshape(columns, leaf_count * leaf)
    return (near + far).astype(jnp.bfloat16)


def solution(mesh):
    placed = (
        P("group", "cluster"),
        P("cluster", "group", None, None),
        P("cluster", None),
        P("cluster", None, None),
        P("cluster", None, None),
        P("cluster", None, None),
        P("cluster", None),
    )
    return jax.shard_map(
        local, mesh=mesh, in_specs=placed, out_specs=P("group", "cluster"), check_vma=False
    )
```

profile of v0, /device:TPU:1, one launch (start us, length us, event | category | flops | bytes accessed | tf_op | source)
XLA Modules:
  0.0 300.0 jit_solution(17901057089317434044)
XLA Ops:
  6.5 0.0 copy-start
  6.5 0.7 all-gather.3.cloned.1.call-update
  7.3 0.0 all-gather.5.cloned.1.call-start
  7.3 1.5 convolution_convert_fusion
  8.8 0.9 reshape.33
  9.7 0.0 all-gather.5.cloned.1.call-update
  9.8 0.0 reduce-scatter.2.cloned.1.call-start
  9.8 38.2 %all-gather.3.cloned.1.call-done = bf16[512,4096]{1,0:T(8,128)(2,1)} async-done(((bf16[64,4096]{1,0:T(8,128)(2,1)}), bf16[512,4096]{1,0:T(8,128)(2,1)}) %all-gather.3.cloned.1.call-update) | async-done | bytes 4194320 | tf_op jit(solution)/shard_map/all_gather | solution.py:35
  48.0 6.5 %copy.20 = bf16[512,4096]{0,1:T(8,128)(2,1)} copy(bf16[512,4096]{1,0:T(8,128)(2,1)} %all-gather.3.cloned.1.call-done) | data formatting | bytes 8388608 | tf_op jit(solution)/shard_map/all_gather | solution.py:35
  54.4 1.2 collective-permute-start
  55.7 4.0 %collective-permute-start.1 = (bf16[512,4096]{0,1:T(8,128)(2,1)}, bf16[512,4096]{0,1:T(8,128)(2,1)}, u32[]{:S(2)}, u32[]{:S(2)}) collective-permute-start(bf16[512,4096]{0,1:T(8,128)(2,1)} %copy.20), channel_id=1, source_target_pairs={{8,0},{16,8},{24,16},{32,24},{40,32},{48,40},{56,48},{64,56},{72,6... | collective-permute-start | bytes 12582920 | tf_op jit(solution)/shard_map/ppermute | solution.py:18
  59.7 0.1 compare_and_fusion.1
  59.8 0.1 reshape.38
  59.9 111.9 %collective-permute-done = bf16[512,4096]{0,1:T(8,128)(2,1)} collective-permute-done((bf16[512,4096]{0,1:T(8,128)(2,1)}, bf16[512,4096]{0,1:T(8,128)(2,1)}, u32[]{:S(2)}, u32[]{:S(2)}) %collective-permute-start) | collective-permute-done | bytes 4194336 | tf_op jit(solution)/shard_map/ppermute | solution.py:16
  171.7 0.0 collective-permute-done.1
  171.7 15.9 %pad_maximum_fusion = bf16[512,12288]{0,1:T(8,128)(2,1)} fusion(bf16[512,4096]{0,1:T(8,128)(2,1)} %collective-permute-done.1, bf16[512,4096]{0,1:T(8,128)(2,1)} %copy.20, bf16[512,4096]{0,1:T(8,128)(2,1)} %collective-permute-done), kind=kLoop, calls=%fused_computation.2 | loop fusion | flops 37748736 | bytes 25165824 | tf_op jit(solution)/shard_map/concatenate | solution.py:14
  187.7 15.9 %copy.23 = bf16[512,48,256]{2,0,1:T(8,128)(2,1)} copy(bf16[512,48,256]{0,2,1:T(8,128)(2,1)} %bitcast.29) | data formatting | bytes 25165824 | tf_op jit(solution)/shard_map/reshape | solution.py:39
  203.5 10.9 %gather_fusion = bf16[48,512,256]{2,1,0:T(8,128)(2,1)} fusion(bf16[512,48,256]{2,0,1:T(8,128)(2,1)} %copy.23, s32[1024]{0:T(1024)S(1)} %pad_clamp_fusion.1), kind=kCustom, calls=%fused_computation | custom fusion | bytes 25166016 | tf_op jit(solution)/shard_map/jit(_take)/gather | solution.py:43
  214.4 10.5 %fusion = f32[16,512,256,1]{1,2,3,0:T(8,128)} fusion(bf16[16,3,256,256]{3,2,1,0:T(8,128)(2,1)} %param.8, bf16[16,3,512,256]{3,2,1,0:T(8,128)(2,1)} %bitcast.30, pred[16,3]{1,0:T(8,128)(4,1)S(1)} %get-tuple-element.5), kind=kOutput, calls=%fused_computation.3 | convolution fusion | flops 3227516928 | bytes 27263024 | tf_op jit(solution)/shard_map/rmkc,mknc->rmn/dot_general | solution.py:44
  224.9 8.9 %copy.24 = f32[512,4096]{1,0:T(8,128)} copy(f32[512,4096]{0,1:T(8,128)} %bitcast.31) | data formatting | bytes 16777216 | tf_op jit(solution)/shard_map/reshape | solution.py:45
  233.9 0.0 reduce-scatter.2.cloned.1.call-update
  233.9 0.7 copy-done.2
  234.6 0.1 reshape.46
  234.6 0.8 copy-done.1
  235.5 4.1 %reshape.34 = bf16[16,64,16,64]{3,2,1,0:T(8,128)(2,1)} reshape(bf16[16,64,1024]{2,1,0:T(8,128)(2,1)S(1)} %copy-done.1) | data formatting | bytes 4194304 | tf_op jit(solution)/shard_map/reshape | solution.py:50
  239.5 0.0 all-gather.5.cloned.1.call-done
  239.6 6.6 %gather_fusion.1 = bf16[256,4096]{1,0:T(8,128)(2,1)S(1)} fusion(bf16[512,4096]{1,0:T(8,128)(2,1)} %all-gather.5.cloned.1.call-done, s32[1024]{0:T(1024)S(1)} %pad_clamp_fusion), kind=kCustom, calls=%fused_computation.1 | custom fusion | bytes 4195328 | tf_op jit(solution)/shard_map/jit(_take)/gather | solution.py:52
  246.2 5.5 %gather.12 = bf16[16,16,64,64]{3,2,1,0:T(8,128)(2,1)} reshape(bf16[256,4096]{1,0:T(8,128)(2,1)S(1)} %gather_fusion.1) | data formatting | bytes 4194304 | tf_op jit(solution)/shard_map/jit(_take)/gather | solution.py:52
  251.7 4.9 %convolution_bitcast_fusion = f32[16,8,8,256]{3,2,1,0:T(8,128)S(1)} fusion(bf16[16,64,256]{2,1,0:T(8,128)(2,1)S(1)} %copy-done, bf16[16,64,16,64]{3,2,1,0:T(8,128)(2,1)} %reshape.34, bf16[16,16,64,64]{3,2,1,0:T(8,128)(2,1)} %gather.12, pred[16,16]{1,0:T(8,128)(4,1)S(1)} %compare_and_fusion), kind=kOutput, calls=%fused_computation.13 | convolution fusion | flops 168886272 | bytes 5767424 | tf_op jit(solution)/shard_map/lrb,lbn->rln/dot_general | solution.py:56
  256.6 0.1 copy.31
  256.7 34.6 %reduce-scatter.2.cloned.1.call-done = f32[64,4096]{1,0:T(8,128)} async-done(((f32[512,4096]{1,0:T(8,128)}), f32[64,4096]{1,0:T(8,128)}) %reduce-scatter.2.cloned.1.call-update) | async-done | bytes 1048592 | tf_op jit(solution)/shard_map/reduce_scatter | solution.py:46
  291.4 2.1 add_convert_fusion
  (10 shorter events, 0.0 us)
Async XLA Ops:
  6.5 245.2 %copy-start = (bf16[16,64,256]{2,1,0:T(8,128)(2,1)S(1)}, bf16[16,64,256]{2,1,0:T(8,128)(2,1)}, u32[]{:S(2)}) copy-start(bf16[16,64,256]{2,1,0:T(8,128)(2,1)} %param.12) | copy-start | bytes 1572868
  6.5 53.1 %copy-start.3 = (s32[16,24]{1,0:T(8,128)S(1)}, s32[16,24]{1,0:T(8,128)}, u32[]{:S(2)}) copy-start(s32[16,24]{1,0:T(8,128)} %param.9) | copy-start | bytes 4612
  6.5 41.5 %all-gather.3.cloned.1.call-start = ((), (), s32[]{:S(2)}) async-start(), calls=%async_computation.1 | async-start | bytes 4718592 | tf_op jit(solution)/shard_map/all_gather | solution.py:35
  7.3 232.3 %all-gather.5.cloned.1.call-start = ((), (), s32[]{:S(2)}) async-start(), calls=%async_computation.3 | async-start | bytes 4325376 | tf_op jit(solution)/shard_map/all_gather | solution.py:51
  9.8 281.6 %reduce-scatter.2.cloned.1.call-start = ((), (), s32[]{:S(2)}) async-start(), calls=%async_computation.2 | async-start | bytes 9437184 | tf_op jit(solution)/shard_map/reduce_scatter | solution.py:46
  54.4 117.3 %collective-permute-start = (bf16[512,4096]{0,1:T(8,128)(2,1)}, bf16[512,4096]{0,1:T(8,128)(2,1)}, u32[]{:S(2)}, u32[]{:S(2)}) collective-permute-start(bf16[512,4096]{0,1:T(8,128)(2,1)} %copy.20), channel_id=1, source_target_pairs={{0,8},{8,16},{16,24},{24,32},{32,40},{40,48},{48,56},{56,64},{64,7... | collective-permute-start | bytes 12582920 | tf_op jit(solution)/shard_map/ppermute | solution.py:16
  55.7 116.1 %collective-permute-start.1 = (bf16[512,4096]{0,1:T(8,128)(2,1)}, bf16[512,4096]{0,1:T(8,128)(2,1)}, u32[]{:S(2)}, u32[]{:S(2)}) collective-permute-start(bf16[512,4096]{0,1:T(8,128)(2,1)} %copy.20), channel_id=1, source_target_pairs={{8,0},{16,8},{24,16},{32,24},{40,32},{48,40},{56,48},{64,56},{72,6... | collective-permute-start | bytes 12582920 | tf_op jit(solution)/shard_map/ppermute | solution.py:18
  233.9 0.7 copy-start.2
  233.9 1.6 copy-start.1
Sparse Core Ops, SparseCore 0:
  9.2 38.7 all-gather.2
  50.6 125.4 all-gather.4
  234.0 57.3 reduce-scatter.1
where the time goes:
time: 301 us; the launch traced here: 300 us
  waiting for transfers between devices  185 us (61%)
  local copies, waits for them, and re-layouts  61 us (20%)
  other arithmetic  18.2 us (6%)
  matrix products  16.9 us (6%)
  between operations  13.2 us (4%)
  starting transfers between devices  5.3 us (2%)
    ppermute x1, waiting for transfers between devices, with_halo(): lax.ppermute(tail, axis, [(i, (i + 1) % count) for i in range(count)])  112 us
    all_gather x1, waiting for transfers between devices, local(): gathered = lax.all_gather(loads, 'group', axis=0, tiled=True)  38.2 us
    reduce_scatter x1, waiting for transfers between devices, local(): lax.psum_scatter(partial_value, 'group', scatter_dimension=0, tiled=True)  34.6 us
    concatenate x1, other arithmetic, with_halo(): jnp.concatenate([lax.ppermute(tail, axis, [(i, (i + 1) % count) for i in...  15.9 us
    reshape x1, local copies, waits for them, and re-layouts, local(): wide_view = widened.reshape(patterns, wide_leaves, leaf)  15.9 us
    gather x2, local copies, waits for them, and re-layouts, local(): chosen = jnp.take(every_coef, far_cols, axis=0)  12.1 us
    gather x1, local copies, waits for them, and re-layouts, local(): picked = jnp.take(wide_view, position, axis=1)  10.9 us
    dot_general x1, matrix products, local(): jnp.einsum('rmkc,mknc->rmn', picked, near_blocks, preferred_element_type=...  10.5 us
  transfers between devices with their start and end apart: 5, of which 3 were waited for; matrix products, arithmetic and copies ran while one was open for 31% of the time, Pallas kernels for 0%

commit v1 on v0

--- a/solution.py
+++ b/solution.py
@@ -32,7 +32,10 @@
     total_leaves = leaf_count * lax.axis_size("cluster")
     cluster_id = lax.axis_index("cluster")
     group_id = lax.axis_index("group")
-    gathered = lax.all_gather(loads, "group", axis=0, tiled=True)
+    draw_the_panels = lambda x_part, shard_axis: jnp.concatenate(
+        lax.all_to_all(jnp.stack([x_part] * lax.axis_size(shard_axis)), shard_axis, 0, 0), axis=0
+    )
+    gathered = draw_the_panels(loads, "group")
     patterns = gathered.shape[0]
     widened = with_halo(gathered, (("cluster", 1),), REACH * leaf)
     wide_leaves = leaf_count + 2 * REACH

time: 301 us -> 312 us (1.037)
  local copies, waits for them, and re-layouts: 61 us -> 74.9 us
  starting transfers between devices: 5.3 us -> 14.1 us
  waiting for transfers between devices: 185 us -> 178 us
  other arithmetic: 18.2 us -> 12.9 us
    all_to_all x0 -> x1, waiting for transfers between devices: none -> 47.5 us  [local(): lax.all_to_all(jnp.stack([x_part] * lax.axis_size(shard_axis)), shard_axi...]
    all_gather x1 -> x0, waiting for transfers between devices: 38.2 us -> none  [local(): gathered = lax.all_gather(loads, 'group', axis=0, tiled=True)]
    concatenate x0 -> x3, local copies, waits for them, and re-layouts: none -> 16 us  [with_halo(): jnp.concatenate([lax.ppermute(tail, axis, [(i, (i + 1) % count) for i in...]
    reshape x1 -> x0, local copies, waits for them, and re-layouts: 15.9 us -> none  [local(): wide_view = widened.reshape(patterns, wide_leaves, leaf)]
    ppermute x0 -> x2, local copies, waits for them, and re-layouts: none -> 13 us  [the longest x1 6.5 us: with_halo(): lax.ppermute(tail, axis, [(i, (i + 1) % count) for i in range(count)])]
    ppermute x1, waiting for transfers between devices: 112 us -> 103 us  [with_halo(): lax.ppermute(tail, axis, [(i, (i + 1) % count) for i in range(count)])]
    all_to_all x0 -> x1, starting transfers between devices: none -> 7.78 us  [local(): lax.all_to_all(jnp.stack([x_part] * lax.axis_size(shard_axis)), shard_axi...]
    reduce_scatter x1, waiting for transfers between devices: 34.6 us -> 27.8 us  [local(): lax.psum_scatter(partial_value, 'group', scatter_dimension=0, tiled=True)]
where the time goes in v1:
time: 312 us; the launch traced here: 311 us
  waiting for transfers between devices  178 us (57%)
  local copies, waits for them, and re-layouts  74.9 us (24%)
  matrix products  15.8 us (5%)
  between operations  14.9 us (5%)
  starting transfers between devices  14.1 us (5%)
  other arithmetic  12.9 us (4%)
    ppermute x1, waiting for transfers between devices, with_halo(): lax.ppermute(tail, axis, [(i, (i + 1) % count) for i in range(count)])  103 us
    all_to_all x1, waiting for transfers between devices, local(): lax.all_to_all(jnp.stack([x_part] * lax.axis_size(shard_axis)), shard_axi...  47.5 us
    reduce_scatter x1, waiting for transfers between devices, local(): lax.psum_scatter(partial_value, 'group', scatter_dimension=0, tiled=True)  27.8 us
    concatenate x3, local copies, waits for them, and re-layouts, with_halo(): jnp.concatenate([lax.ppermute(tail, axis, [(i, (i + 1) % count) for i in...  16 us
    gather x2, local copies, waits for them, and re-layouts, local(): chosen = jnp.take(every_coef, far_cols, axis=0)  12.2 us
    gather x1, local copies, waits for them, and re-layouts, local(): picked = jnp.take(wide_view, position, axis=1)  10.8 us
    concatenate x1, other arithmetic, with_halo(): jnp.concatenate([lax.ppermute(tail, axis, [(i, (i + 1) % count) for i in...  10.7 us
    dot_general x1, matrix products, local(): jnp.einsum('rmkc,mknc->rmn', picked, near_blocks, preferred_element_type=...  10.6 us
  transfers between devices with their start and end apart: 5, of which 3 were waited for; matrix products, arithmetic and copies ran while one was open for 31% of the time, Pallas kernels for 0%

profile of v1, /device:TPU:1, one launch (start us, length us, event | category | flops | bytes accessed | tf_op | source)
XLA Modules:
  0.0 310.7 jit_solution(885359490152451527)
XLA Ops:
  7.4 3.6 %stack.2 = bf16[8,64,4096]{2,1,0:T(8,128)(2,1)} broadcast(bf16[64,4096]{1,0:T(8,128)(2,1)} %param.7), dimensions={1,2} | broadcast | bytes 4718592 | tf_op jit(solution)/shard_map/stack | solution.py:36
  11.0 7.8 %all-to-all-start = ((bf16[8,64,4096]{2,1,0:T(8,128)(2,1)}), bf16[8,64,4096]{2,1,0:T(8,128)(2,1)}, u32[]{:S(2)}, u32[]{:S(2)}) async-start(bf16[8,64,4096]{2,1,0:T(8,128)(2,1)} %stack.2), calls=%async_computation | async-start | bytes 8388608 | tf_op jit(solution)/shard_map/all_to_all | solution.py:36
  18.8 0.3 convolution_convert_fusion
  19.1 0.9 reshape.40
  20.0 0.0 reduce-scatter.2.cloned.1.call-start
  20.1 47.5 %all-to-all-done = bf16[8,64,4096]{2,1,0:T(8,128)(2,1)} async-done(((bf16[8,64,4096]{2,1,0:T(8,128)(2,1)}), bf16[8,64,4096]{2,1,0:T(8,128)(2,1)}, u32[]{:S(2)}, u32[]{:S(2)}) %all-to-all-start) | async-done | bytes 4194336 | tf_op jit(solution)/shard_map/all_to_all | solution.py:36
  67.6 6.3 %collective-permute-start.1 = (bf16[512,4096]{1,0:T(8,128)(2,1)}, bf16[512,4096]{1,0:T(8,128)(2,1)}, u32[]{:S(2)}, u32[]{:S(2)}) collective-permute-start(bf16[512,4096]{1,0:T(8,128)(2,1)} %bitcast), channel_id=1, source_target_pairs={{8,0},{16,8},{24,16},{32,24},{40,32},{48,40},{56,48},{64,56},{72,6... | collective-permute-start | bytes 12582920 | tf_op jit(solution)/shard_map/ppermute | solution.py:18
  73.9 0.1 compare_and_fusion.1
  74.0 0.1 reshape.45
  74.1 3.6 %copy.34 = bf16[64,8,16,256]{3,2,1,0:T(8,128)(2,1)S(1)} copy(bf16[64,8,16,256]{3,1,2,0:T(8,128)(2,1)} %bitcast.19) | data formatting | bytes 8388608
  77.7 3.5 %copy.24 = bf16[512,16,256]{2,0,1:T(8,128)(2,1)} copy(bf16[512,16,256]{2,1,0:T(8,128)(2,1)S(1)} %bitcast.37) | data formatting | bytes 8388608 | tf_op jit(solution)/shard_map/concatenate | solution.py:14
  81.2 102.7 %collective-permute-done = bf16[512,4096]{1,0:T(8,128)(2,1)} collective-permute-done((bf16[512,4096]{1,0:T(8,128)(2,1)}, bf16[512,4096]{1,0:T(8,128)(2,1)}, u32[]{:S(2)}, u32[]{:S(2)}) %collective-permute-start) | collective-permute-done | bytes 4194336 | tf_op jit(solution)/shard_map/ppermute | solution.py:16
  183.9 6.5 %copy.21 = bf16[512,4096]{0,1:T(8,128)(2,1)} copy(bf16[512,4096]{1,0:T(8,128)(2,1)} %collective-permute-done) | data formatting | bytes 8388608 | tf_op jit(solution)/shard_map/ppermute | solution.py:16
  190.3 6.3 %copy.23 = bf16[512,16,256]{2,0,1:T(8,128)(2,1)} copy(bf16[512,16,256]{0,2,1:T(8,128)(2,1)} %bitcast.35) | data formatting | bytes 8388608 | tf_op jit(solution)/shard_map/concatenate | solution.py:14
  196.7 6.5 %copy.22 = bf16[512,4096]{0,1:T(8,128)(2,1)} copy(bf16[512,4096]{1,0:T(8,128)(2,1)} %collective-permute-done.1) | data formatting | bytes 8388608 | tf_op jit(solution)/shard_map/ppermute | solution.py:18
  203.1 6.3 %copy.25 = bf16[512,16,256]{2,0,1:T(8,128)(2,1)} copy(bf16[512,16,256]{0,2,1:T(8,128)(2,1)} %bitcast.36) | data formatting | bytes 8388608 | tf_op jit(solution)/shard_map/concatenate | solution.py:14
  209.4 10.7 %pad_maximum_fusion = bf16[512,48,256]{2,0,1:T(8,128)(2,1)} fusion(bf16[512,16,256]{2,0,1:T(8,128)(2,1)} %copy.25, bf16[512,16,256]{2,0,1:T(8,128)(2,1)} %copy.24, bf16[512,16,256]{2,0,1:T(8,128)(2,1)} %copy.23), kind=kLoop, calls=%fused_computation.2 | loop fusion | flops 12582912 | bytes 25165824 | tf_op jit(solution)/shard_map/concatenate | solution.py:14
  220.1 10.8 %gather_fusion = bf16[48,512,256]{2,1,0:T(8,128)(2,1)} fusion(bf16[512,48,256]{2,0,1:T(8,128)(2,1)} %pad_maximum_fusion, s32[1024]{0:T(1024)S(1)} %pad_clamp_fusion.1), kind=kCustom, calls=%fused_computation | custom fusion | bytes 25166016 | tf_op jit(solution)/shard_map/jit(_take)/gather | solution.py:46
  231.0 10.6 %fusion = f32[16,512,256,1]{1,2,3,0:T(8,128)} fusion(bf16[16,3,256,256]{3,2,1,0:T(8,128)(2,1)} %param.8, bf16[16,3,512,256]{3,2,1,0:T(8,128)(2,1)} %bitcast.34, pred[16,3]{1,0:T(8,128)(4,1)S(1)} %get-tuple-element.5), kind=kOutput, calls=%fused_computation.3 | convolution fusion | flops 3227516928 | bytes 27263024 | tf_op jit(solution)/shard_map/rmkc,mknc->rmn/dot_general | solution.py:47
  241.5 8.9 %copy.26 = f32[512,4096]{1,0:T(8,128)} copy(f32[512,4096]{0,1:T(8,128)} %bitcast.38) | data formatting | bytes 16777216 | tf_op jit(solution)/shard_map/reshape | solution.py:48
  250.4 0.0 reduce-scatter.2.cloned.1.call-update
  250.5 0.7 copy-done.4
  251.1 0.1 reshape.53
  251.2 0.8 copy-done.1
  252.0 3.9 %reshape.41 = bf16[16,64,16,64]{3,2,1,0:T(8,128)(2,1)} reshape(bf16[16,64,1024]{2,1,0:T(8,128)(2,1)S(1)} %copy-done.1) | data formatting | bytes 4194304 | tf_op jit(solution)/shard_map/reshape | solution.py:53
  256.0 0.0 all-gather.2.cloned.1.call-done
  256.0 6.7 %gather_fusion.1 = bf16[256,4096]{1,0:T(8,128)(2,1)S(1)} fusion(bf16[512,4096]{1,0:T(8,128)(2,1)} %all-gather.2.cloned.1.call-done, s32[1024]{0:T(1024)S(1)} %pad_clamp_fusion), kind=kCustom, calls=%fused_computation.1 | custom fusion | bytes 4195328 | tf_op jit(solution)/shard_map/jit(_take)/gather | solution.py:55
  262.7 5.5 %gather.12 = bf16[16,16,64,64]{3,2,1,0:T(8,128)(2,1)} reshape(bf16[256,4096]{1,0:T(8,128)(2,1)S(1)} %gather_fusion.1) | data formatting | bytes 4194304 | tf_op jit(solution)/shard_map/jit(_take)/gather | solution.py:55
  268.3 5.0 %convolution_bitcast_fusion = f32[16,8,8,256]{3,2,1,0:T(8,128)S(1)} fusion(bf16[16,64,256]{2,1,0:T(8,128)(2,1)S(1)} %copy-done, bf16[16,64,16,64]{3,2,1,0:T(8,128)(2,1)} %reshape.41, bf16[16,16,64,64]{3,2,1,0:T(8,128)(2,1)} %gather.12, pred[16,16]{1,0:T(8,128)(4,1)S(1)} %compare_and_fusion), kind=kOutput, calls=%fused_computation.13 | convolution fusion | flops 168886272 | bytes 5767424 | tf_op jit(solution)/shard_map/lrb,lbn->rln/dot_general | solution.py:59
  273.3 0.1 copy.33
  273.4 27.8 %reduce-scatter.2.cloned.1.call-done = f32[64,4096]{1,0:T(8,128)} async-done(((f32[512,4096]{1,0:T(8,128)}), f32[64,4096]{1,0:T(8,128)}) %reduce-scatter.2.cloned.1.call-update) | async-done | bytes 1048592 | tf_op jit(solution)/shard_map/reduce_scatter | solution.py:49
  301.1 2.1 add_convert_fusion
  (18 shorter events, 0.1 us)
Async XLA Ops:
  7.4 260.9 %copy-start = (bf16[16,64,256]{2,1,0:T(8,128)(2,1)S(1)}, bf16[16,64,256]{2,1,0:T(8,128)(2,1)}, u32[]{:S(2)}) copy-start(bf16[16,64,256]{2,1,0:T(8,128)(2,1)} %param.12) | copy-start | bytes 1572868
  11.0 7.8 %copy-start.2 = (bf16[64,4096]{1,0:T(8,128)(2,1)S(1)}, bf16[64,4096]{1,0:T(8,128)(2,1)}, u32[]{:S(2)}) copy-start(bf16[64,4096]{1,0:T(8,128)(2,1)} %param.7) | copy-start | bytes 1572868
  11.0 7.8 %copy-start.3 = (bf16[16,64,256]{2,1,0:T(8,128)(2,1)S(1)}, bf16[16,64,256]{2,1,0:T(8,128)(2,1)}, u32[]{:S(2)}) copy-start(bf16[16,64,256]{2,1,0:T(8,128)(2,1)} %param.10) | copy-start | bytes 1572868
  11.0 62.9 %copy-start.5 = (s32[16,24]{1,0:T(8,128)S(1)}, s32[16,24]{1,0:T(8,128)}, u32[]{:S(2)}) copy-start(s32[16,24]{1,0:T(8,128)} %param.9) | copy-start | bytes 4612
  11.0 56.6 %all-to-all-start = ((bf16[8,64,4096]{2,1,0:T(8,128)(2,1)}), bf16[8,64,4096]{2,1,0:T(8,128)(2,1)}, u32[]{:S(2)}, u32[]{:S(2)}) async-start(bf16[8,64,4096]{2,1,0:T(8,128)(2,1)} %stack.2), calls=%async_computation | async-start | bytes 8388608 | tf_op jit(solution)/shard_map/all_to_all | solution.py:36
  18.8 237.3 %all-gather.2.cloned.1.call-start = ((), (), s32[]{:S(2)}) async-start(), calls=%async_computation.3 | async-start | bytes 4325376 | tf_op jit(solution)/shard_map/all_gather | solution.py:54
  20.0 281.1 %reduce-scatter.2.cloned.1.call-start = ((), (), s32[]{:S(2)}) async-start(), calls=%async_computation.2 | async-start | bytes 9437184 | tf_op jit(solution)/shard_map/reduce_scatter | solution.py:49
  67.6 116.3 %collective-permute-start = (bf16[512,4096]{1,0:T(8,128)(2,1)}, bf16[512,4096]{1,0:T(8,128)(2,1)}, u32[]{:S(2)}, u32[]{:S(2)}) collective-permute-start(bf16[512,4096]{1,0:T(8,128)(2,1)} %bitcast), channel_id=1, source_target_pairs={{0,8},{8,16},{16,24},{24,32},{32,40},{40,48},{48,56},{56,64},{64,7... | collective-permute-start | bytes 12582920 | tf_op jit(solution)/shard_map/ppermute | solution.py:16
  67.6 129.1 %collective-permute-start.1 = (bf16[512,4096]{1,0:T(8,128)(2,1)}, bf16[512,4096]{1,0:T(8,128)(2,1)}, u32[]{:S(2)}, u32[]{:S(2)}) collective-permute-start(bf16[512,4096]{1,0:T(8,128)(2,1)} %bitcast), channel_id=1, source_target_pairs={{8,0},{16,8},{24,16},{32,24},{40,32},{48,40},{56,48},{64,56},{72,6... | collective-permute-start | bytes 12582920 | tf_op jit(solution)/shard_map/ppermute | solution.py:18
  250.4 0.7 copy-start.4
  250.4 1.6 copy-start.1
Sparse Core Ops, SparseCore 0:
  22.1 139.7 all-gather.1
Sparse Core Ops, SparseCore 1:
  250.5 50.5 reduce-scatter.1
